TPU v7x, 256 devices: a whole 4x4x8 slice. The times are simulated.
256 devices in a mesh: dp: 32 (over z_lo, y, x), seq: 8 (over z_hi, core).
Axes of the slice: x: 4, y: 4, z: 8 (z_hi: 4, z_lo: 2; z = z_hi * 2 + z_lo), core: 2. Of those that a mesh axis runs over, the one named last changes fastest.
Arguments:
- tokens: bfloat16 [32, 1024, 1024], P('dp', 'seq'), may hold values from -6 to 6
- positions: int32 [32, 1024], P('dp', 'seq'), may hold values from 0 to 4095
- counts: int32 [32, 8], P('dp'), may hold values from 1 to 128, 768 in all within a row
- ln_gain: float32 [1024], replicated, may hold values from 0.1 to 1.9
- w_qkv: bfloat16 [3, 1024, 1024], replicated
- w_out: bfloat16 [1024, 1024], replicated, may hold values from -0.1875 to 0.1875
- d_out: bfloat16 [32, 1024, 1024], P('dp', 'seq'), may hold values from -6 to 6
Outputs:
- d_tokens: bfloat16 [32, 1024, 1024], P('dp', 'seq')
- grad_qkv: float32 [3, 1024, 1024], P(None, 'seq', 'dp')
- grad_out: float32 [1024, 1024], P('dp', 'seq')
Inputs may be any that keep to these rules, and one draw needn't show every extreme that they name: Each record's counts sum to 768, and the largest of them is 128.
All inputs are finite; a program needn't handle non-finite values.
Results may differ from a plain program's by a relative error of at most 0.0075.
Values may be sent and summed in bfloat16 or wider, within the bound.
A program may use at most 128 MiB of HBM per device.

v0:
```python
import math

import jax
import jax.numpy as jnp
from jax import lax
from jax.sharding import PartitionSpec as P

HEAD_DIM = 64


EPSILON = 1e-06
MASKED = -1e30


def position_code(places, feature_width):
    half = feature_width // 2
    freqs = jnp.exp(jnp.arange(half, dtype=jnp.float32) * (-math.log(10000.0) / half))
    angle = places.astype(jnp.float32)[:, None] * freqs[None, :]
    return jnp.concatenate([jnp.sin(angle), jnp.cos(angle)], axis=1)


def layer_norm(inputs, places, ln_gain):
    shifted = inputs.astype(jnp.float32) + position_code(places, inputs.shape[1])
    centred = shifted - jnp.mean(shifted, axis=1, keepdims=True)
    inv_std = lax.rsqrt(jnp.mean(centred * centred, axis=1, keepdims=True) + EPSILON)
    standard = centred * inv_std
    normed = (standard * ln_gain).astype(jnp.bfloat16)
    return (normed, standard, inv_std)


def input_grad(query_grad, key_grad, value_grad, masked_grad, w_qkv, standard, inv_std, ln_gain):
    normed_grad = jnp.dot(query_grad, w_qkv[0], preferred_element_type=jnp.float32)
    normed_grad = normed_grad + jnp.dot(key_grad, w_qkv[1], preferred_element_type=jnp.float32)
    normed_grad = normed_grad + jnp.dot(value_grad, w_qkv[2], preferred_element_type=jnp.float32)
    unit_grad = normed_grad * ln_gain
    inner = unit_grad - jnp.mean(unit_grad, axis=1, keepdims=True)
    inner = inner - standard * jnp.mean(unit_grad * standard, axis=1, keepdims=True)
    return (masked_grad.astype(jnp.float32) + inv_std * inner).astype(jnp.bfloat16)


def project(normed, weight):
    return jnp.einsum("td,od->to", normed, weight, preferred_element_type=jnp.float32).astype(
        jnp.bfloat16
    )


def token_sum(left, right):
    return lax.dot_general(
        left, right, (((0,), (0,)), ((), ())), preferred_element_type=jnp.float32
    )


def attention_grads(queries, key_rows, value_rows, attn_grad, key_valid, score_scale):
    total, span = queries.shape
    heads_here = span // HEAD_DIM
    block = math.gcd(512, total)
    blocks = total // block
    key_three = key_rows.reshape(total, heads_here, HEAD_DIM)
    value_three = value_rows.reshape(total, heads_here, HEAD_DIM)
    query_four = queries.reshape(blocks, block, heads_here, HEAD_DIM)
    grad_four = attn_grad.reshape(blocks, block, heads_here, HEAD_DIM)

    def step(carry, item):
        key_acc, value_acc = carry
        query_block, grad_block = item
        scores = (
            jnp.einsum("qhd,khd->hqk", query_block, key_three, preferred_element_type=jnp.float32)
            * score_scale
        )
        scores = jnp.where(key_valid[None, None, :], scores, MASKED)
        peak = jnp.max(scores, axis=2, keepdims=True)
        expo = jnp.exp(scores - peak)
        probs = expo / jnp.sum(expo, axis=2, keepdims=True)
        probs_low = probs.astype(jnp.bfloat16)
        attended = jnp.einsum(
            "hqk,khd->qhd", probs_low, value_three, preferred_element_type=jnp.float32
        )
        delta = jnp.sum(grad_block.astype(jnp.float32) * attended, axis=2)
        prob_grad = jnp.einsum(
            "qhd,khd->hqk", grad_block, value_three, preferred_element_type=jnp.float32
        )
        score_grad = (probs * (prob_grad - jnp.transpose(delta)[:, :, None])).astype(jnp.bfloat16)
        query_grad = jnp.einsum(
            "hqk,khd->qhd", score_grad, key_three, preferred_element_type=jnp.float32
        )
        query_grad = (query_grad * score_scale).astype(jnp.bfloat16)
        key_acc = key_acc + jnp.einsum(
            "hqk,qhd->khd", score_grad, query_block, preferred_element_type=jnp.float32
        )
        value_acc = value_acc + jnp.einsum(
            "hqk,qhd->khd", probs_low, grad_block, preferred_element_type=jnp.float32
        )
        return ((key_acc, value_acc), (attended.astype(jnp.bfloat16), query_grad))

    zeros_acc = jnp.zeros((total, heads_here, HEAD_DIM), jnp.float32)
    sums, outputs = lax.scan(step, (zeros_acc, zeros_acc), (query_four, grad_four))
    attended = outputs[0].reshape(total, span)
    query_grad = outputs[1].reshape(total, span)
    key_grad = (sums[0] * score_scale).astype(jnp.bfloat16).reshape(total, span)
    value_grad = sums[1].astype(jnp.bfloat16).reshape(total, span)
    return (attended, query_grad, key_grad, value_grad)


def shards(tokens, positions, counts, ln_gain, w_qkv, w_out, d_out):
    inputs = tokens[0]
    places = positions[0]
    upstream = d_out[0]
    capacity, feature_width = inputs.shape
    shard_total = lax.axis_size("seq")
    shard_index = lax.axis_index("seq")
    slot_count = capacity * shard_total
    key_valid = jnp.arange(slot_count, dtype=jnp.int32) % capacity < jnp.repeat(counts[0], capacity)
    own_valid = lax.dynamic_slice_in_dim(key_valid, shard_index * capacity, capacity)
    normed, standard, inv_std = layer_norm(inputs, places, ln_gain)
    masked_grad = jnp.where(own_valid[:, None], upstream, jnp.zeros_like(upstream))
    score_scale = HEAD_DIM ** (-0.5)
    factor = 1.0 / math.sqrt(lax.axis_size("dp") * (3 * slot_count // 4))
    queries = project(normed, w_qkv[0])
    key_rows = project(normed, w_qkv[1])
    value_rows = project(normed, w_qkv[2])
    attn_grad = jnp.dot(masked_grad, w_out, preferred_element_type=jnp.float32).astype(jnp.bfloat16)
    head_query, head_key, head_value, head_grad = (
        lax.all_to_all(queries, "seq", split_axis=1, concat_axis=0, tiled=True),
        lax.all_to_all(key_rows, "seq", split_axis=1, concat_axis=0, tiled=True),
        lax.all_to_all(value_rows, "seq", split_axis=1, concat_axis=0, tiled=True),
        lax.all_to_all(attn_grad, "seq", split_axis=1, concat_axis=0, tiled=True),
    )
    attended, query_grad, key_grad, value_grad = attention_grads(
        head_query, head_key, head_value, head_grad, key_valid, score_scale
    )
    attended_rows, query_rows, key_back, value_back = (
        lax.all_to_all(attended, "seq", split_axis=0, concat_axis=1, tiled=True),
        lax.all_to_all(query_grad, "seq", split_axis=0, concat_axis=1, tiled=True),
        lax.all_to_all(key_grad, "seq", split_axis=0, concat_axis=1, tiled=True),
        lax.all_to_all(value_grad, "seq", split_axis=0, concat_axis=1, tiled=True),
    )
    term_qkv = jnp.stack(
        [token_sum(query_rows, normed), token_sum(key_back, normed), token_sum(value_back, normed)]
    )
    term_out = token_sum(masked_grad, attended_rows)
    part_qkv, part_out = (
        lax.psum_scatter(term_qkv, "dp", scatter_dimension=2, tiled=True),
        lax.psum_scatter(term_out, "dp", scatter_dimension=0, tiled=True),
    )
    grad_qkv, grad_out = (
        lax.psum_scatter(part_qkv, "seq", scatter_dimension=1, tiled=True),
        lax.psum_scatter(part_out, "seq", scatter_dimension=1, tiled=True),
    )
    d_inputs = input_grad(
        query_rows, key_back, value_back, masked_grad, w_qkv, standard, inv_std, ln_gain
    )
    return (d_inputs[None], grad_qkv * factor, grad_out * factor)


def solution(mesh):
    placed = (
        P("dp", "seq", None),
        P("dp", "seq"),
        P("dp", None),
        P(),
        P(),
        P(),
        P("dp", "seq", None),
    )
    return jax.shard_map(
        shards,
        mesh=mesh,
        in_specs=placed,
        out_specs=(P("dp", "seq", None), P(None, "seq", "dp"), P("dp", "seq")),
        check_vma=False,
    )
```

profile of v0, /device:TPU:1, one launch (start us, length us, event | category | flops | bytes accessed | tf_op | source)
XLA Modules:
  0.0 788.1 jit_solution(9005553400882176612)
XLA Ops:
  8.8 1.4 convolution_convert_fusion
  11.1 9.9 %all-to-all-start.2 = ((bf16[128,8,128]{0,2,1:T(8,128)(2,1)}), bf16[128,8,128]{0,2,1:T(8,128)(2,1)S(1)}, u32[]{:S(2)}, u32[]{:S(2)}) async-start(bf16[128,8,128]{0,2,1:T(8,128)(2,1)} %bitcast.11), calls=%async_computation.2 | async-start | bytes 524288 | tf_op jit(solution)/shard_map/all_to_all | solution.py:126
  24.2 2.4 fusion.81
  27.4 3.0 all-to-all-done.2
  30.3 6.4 all-to-all-start.3
  36.7 2.4 fusion.84
  39.9 7.5 all-to-all-done.3
  47.4 4.0 all-to-all-start.1
  51.4 2.4 fusion.72
  54.7 6.1 all-to-all-done.1
  60.7 6.6 all-to-all-start
  68.3 1.8 reshape.297
  71.9 1.1 reshape.298
  73.8 1.1 reshape.296
  74.9 2.6 all-to-all-done
  78.3 1.8 reshape.295
  81.1 23.0 %while.17 = (s32[]{:T(128)}, f32[1024,2,64]{0,2,1:T(8,128)S(1)}, f32[1024,2,64]{0,2,1:T(8,128)S(1)}, bf16[2,512,2,64]{1,3,2,0:T(8,128)(2,1)}, bf16[2,512,2,64]{1...) while((s32[]{:T(128)}, f32[1024,2,64]{0,2,1:T(8,128)S(1)}, ...), condition=%wide.region_6.7_spmd.clone, body=%wide.region_2.6_spmd.clone.sunk | while | flops 816716800 | bytes 50485580 | solution.py:96
  81.2 3.4 fusion.166
  84.5 2.7 fusion.167
  92.7 3.4 fusion.166
  96.0 2.7 fusion.167
  104.1 1.2 copy.88
  105.5 14.0 %all_to_all.140 = bf16[8,128,128]{1,2,0:T(8,128)(2,1)S(1)} all-to-all(bf16[8,128,128]{1,2,0:T(8,128)(2,1)S(1)} %copy.89), channel_id=1, replica_groups=mesh['dp'=32,'seq'=8] {'seq'}, dimensions={0} | all-to-all | bytes 524288 | tf_op jit(solution)/shard_map/all_to_all | solution.py:132
  119.5 3.9 fusion.94
  124.6 6.6 all-to-all-start.4
  132.0 10.7 %all-to-all-done.4 = bf16[8,128,128]{1,2,0:T(8,128)(2,1)S(1)} async-done(((bf16[8,128,128]{1,2,0:T(8,128)(2,1)}), bf16[8,128,128]{1,2,0:T(8,128)(2,1)S(1)}, u32[]{:S(2)}, u32[]{:S(2)}) %all-to-all-start.4) | async-done | bytes 262176 | tf_op jit(solution)/shard_map/all_to_all | solution.py:133
  142.7 5.3 all-to-all-start.5
  148.8 10.4 %all-to-all-done.5 = bf16[8,128,128]{1,2,0:T(8,128)(2,1)S(1)} async-done(((bf16[8,128,128]{1,2,0:T(8,128)(2,1)}), bf16[8,128,128]{1,2,0:T(8,128)(2,1)S(1)}, u32[]{:S(2)}, u32[]{:S(2)}) %all-to-all-start.5) | async-done | bytes 262176 | tf_op jit(solution)/shard_map/all_to_all | solution.py:134
  159.3 5.3 all-to-all-start.6
  164.5 2.6 convolution_bitcast_fusion.5
  167.2 2.6 convolution_bitcast_fusion.4
  169.8 8.2 %all-to-all-done.6 = bf16[8,128,128]{1,2,0:T(8,128)(2,1)S(1)} async-done(((bf16[8,128,128]{1,2,0:T(8,128)(2,1)}), bf16[8,128,128]{1,2,0:T(8,128)(2,1)S(1)}, u32[]{:S(2)}, u32[]{:S(2)}) %all-to-all-start.6) | async-done | bytes 262176 | tf_op jit(solution)/shard_map/all_to_all | solution.py:135
  178.7 1.5 copy-done.3
  180.2 6.5 pad_maximum_fusion
  186.7 18.4 %copy.87 = f32[3,1024,1024]{1,0,2:T(4,128)} copy(f32[3,1024,1024]{2,1,0:T(8,128)} %pad_maximum_fusion) | data formatting | bytes 25165824 | tf_op jit(solution)/shard_map/stack | solution.py:137
  207.1 2.9 fusion.45
  210.0 66.9 %reduce-scatter.6.cloned.1.call-done = f32[32,1024]{1,0:T(8,128)} async-done(((f32[1024,1024]{1,0:T(8,128)}), f32[32,1024]{1,0:T(8,128)}) %reduce-scatter.6.cloned.1.call-update) | async-done | bytes 131088 | tf_op jit(solution)/shard_map/reduce_scatter | solution.py:143
  276.9 2.9 fusion.49
  279.8 419.0 %all-reduce.3.cloned.1.call-done = f32[3,1024,1024]{1,0,2:T(4,128)} async-done(((f32[3,1024,1024]{1,0,2:T(4,128)}), f32[3,1024,1024]{1,0,2:T(4,128)}) %all-reduce.3.cloned.1.call-update) | async-done | bytes 12582928
  698.7 1.1 constant_dynamic-slice_fusion
  699.9 13.7 %copy.93 = f32[3,1024,32]{0,2,1:T(8,128)} copy(f32[3,1024,32]{1,0,2:T(4,128)S(1)} %constant_dynamic-slice_fusion) | data formatting | bytes 786432
  713.6 15.4 %reshape.304 = f32[1024,96]{1,0:T(8,128)} reshape(f32[1024,32,3]{2,1,0:T(8,128)} %bitcast.225) | data formatting | bytes 786432
  729.0 2.6 fusion.106
  732.6 3.2 reduce-scatter.8.cloned.1.call-done
  735.8 1.3 broadcast_multiply_fusion.1
  737.1 36.8 %reduce-scatter.10.cloned.1.call-done = f32[128,96]{1,0:T(8,128)} async-done(((f32[1024,96]{1,0:T(8,128)}), f32[128,96]{1,0:T(8,128)}) %reduce-scatter.10.cloned.1.call-update) | async-done | bytes 49168
  773.9 4.3 reshape.305
  778.3 2.7 copy.94
  (101 shorter events, 30.8 us)
Async XLA Ops:
  7.2 1.6 copy-start
  7.2 16.5 %copy-start.4 = (bf16[1,128,1024]{2,1,0:T(8,128)(2,1)S(1)}, bf16[1,128,1024]{2,1,0:T(8,128)(2,1)}, u32[]{:S(2)}) copy-start(bf16[1,128,1024]{2,1,0:T(8,128)(2,1)} %param.9) | copy-start | bytes 786436
  7.2 16.8 %copy-start.11 = (f32[1024]{0:T(1024)S(1)}, f32[1024]{0:T(1024)}, u32[]{:S(2)}) copy-start(f32[1024]{0:T(1024)} %param.12) | copy-start | bytes 12292
  11.1 19.3 %all-to-all-start.2 = ((bf16[128,8,128]{0,2,1:T(8,128)(2,1)}), bf16[128,8,128]{0,2,1:T(8,128)(2,1)S(1)}, u32[]{:S(2)}, u32[]{:S(2)}) async-start(bf16[128,8,128]{0,2,1:T(8,128)(2,1)} %bitcast.11), calls=%async_computation.2 | async-start | bytes 524288 | tf_op jit(solution)/shard_map/all_to_all | solution.py:126
  30.3 17.1 %all-to-all-start.3 = ((bf16[128,8,128]{2,0,1:T(8,128)(2,1)}), bf16[128,8,128]{2,0,1:T(8,128)(2,1)S(1)}, u32[]{:S(2)}, u32[]{:S(2)}) async-start(bf16[128,8,128]{2,0,1:T(8,128)(2,1)} %bitcast.185), calls=%async_computation.3 | async-start | bytes 524288 | tf_op jit(solution)/shard_map/all_to_all | solution.py:125
  47.4 13.3 %all-to-all-start.1 = ((bf16[128,8,128]{2,0,1:T(8,128)(2,1)}), bf16[128,8,128]{2,0,1:T(8,128)(2,1)S(1)}, u32[]{:S(2)}, u32[]{:S(2)}) async-start(bf16[128,8,128]{2,0,1:T(8,128)(2,1)} %bitcast.186), calls=%async_computation.1 | async-start | bytes 524288 | tf_op jit(solution)/shard_map/all_to_all | solution.py:124
  51.4 29.7 %copy-start.12 = (s32[1,8]{1,0:T(1,128)S(1)}, s32[1,8]{1,0:T(1,128)}, u32[]{:S(2)}) copy-start(s32[1,8]{1,0:T(1,128)} %param.11) | copy-start | bytes 100
  60.7 16.7 %all-to-all-start = ((bf16[128,8,128]{0,2,1:T(8,128)(2,1)}), bf16[128,8,128]{0,2,1:T(8,128)(2,1)S(1)}, u32[]{:S(2)}, u32[]{:S(2)}) async-start(bf16[128,8,128]{0,2,1:T(8,128)(2,1)} %bitcast.7), calls=%async_computation | async-start | bytes 524288 | tf_op jit(solution)/shard_map/all_to_all | solution.py:123
  67.4 209.5 %reduce-scatter.6.cloned.1.call-start = ((), (), s32[]{:S(2)}) async-start(), calls=%async_computation.11 | async-start | bytes 4325376 | tf_op jit(solution)/shard_map/reduce_scatter | solution.py:143
  87.3 2.2 copy-start.2
  89.4 0.9 copy-start.6
  90.4 1.3 copy-start.9
  91.2 0.7 copy-start.7
  91.9 0.7 copy-start.10
  98.7 2.2 copy-start.2
  100.9 0.9 copy-start.6
  101.9 1.3 copy-start.9
  102.6 0.7 copy-start.7
  103.4 0.7 copy-start.10
  119.5 3.9 copy-start.8
  124.6 18.1 %all-to-all-start.4 = ((bf16[8,128,128]{1,2,0:T(8,128)(2,1)}), bf16[8,128,128]{1,2,0:T(8,128)(2,1)S(1)}, u32[]{:S(2)}, u32[]{:S(2)}) async-start(bf16[8,128,128]{1,2,0:T(8,128)(2,1)} %copy.84), calls=%async_computation.4 | async-start | bytes 524288 | tf_op jit(solution)/shard_map/all_to_all | solution.py:133
  142.7 16.5 %all-to-all-start.5 = ((bf16[8,128,128]{1,2,0:T(8,128)(2,1)}), bf16[8,128,128]{1,2,0:T(8,128)(2,1)S(1)}, u32[]{:S(2)}, u32[]{:S(2)}) async-start(bf16[8,128,128]{1,2,0:T(8,128)(2,1)} %copy.85), calls=%async_computation.5 | async-start | bytes 524288 | tf_op jit(solution)/shard_map/all_to_all | solution.py:134
  159.3 18.8 %all-to-all-start.6 = ((bf16[8,128,128]{1,2,0:T(8,128)(2,1)}), bf16[8,128,128]{1,2,0:T(8,128)(2,1)S(1)}, u32[]{:S(2)}, u32[]{:S(2)}) async-start(bf16[8,128,128]{1,2,0:T(8,128)(2,1)} %copy.86), calls=%async_computation.6 | async-start | bytes 524288 | tf_op jit(solution)/shard_map/all_to_all | solution.py:135
  164.5 534.2 %all-reduce.3.cloned.1.call-start = ((), (), s32[]{:S(2)}) async-start(), calls=%async_computation.14 | async-start | bytes 33554432
  178.0 2.2 copy-start.3
  205.2 0.7 copy-start.13
  205.2 530.6 %reduce-scatter.8.cloned.1.call-start = ((), (), s32[]{:S(2)}) async-start(), calls=%async_computation.12 | async-start | bytes 147456 | tf_op jit(solution)/shard_map/reduce_scatter | solution.py:147
  276.9 497.1 %reduce-scatter.10.cloned.1.call-start = ((), (), s32[]{:S(2)}) async-start(), calls=%async_computation.13 | async-start | bytes 589824
  729.0 2.7 copy-start.5
  729.0 52.6 %copy-start.1 = (bf16[1024,1024]{1,0:T(8,128)(2,1)S(1)}, bf16[1024,1024]{1,0:T(8,128)(2,1)}, u32[]{:S(2)}) copy-start(bf16[1024,1024]{1,0:T(8,128)(2,1)} %param.14) | copy-start | bytes 6291460
Sparse Core Ops, SparseCore 0:
  123.5 153.2 reduce-scatter.5
  279.5 419.1 all-reduce.2
  701.2 34.5 reduce-scatter.7
  738.2 35.6 reduce-scatter.9
where the time goes:
time: 792 us; the launch traced here: 788 us
  waiting for transfers between devices  574 us (72%)
  local copies, waits for them, and re-layouts  81.7 us (10%)
  starting transfers between devices  44.1 us (6%)
  matrix products  40.6 us (5%)
  other arithmetic  18.5 us (2%)
  between operations  14.7 us (2%)
  blocking collectives  14 us (2%)
    unnamed x6, waiting for transfers between devices  456 us
    reduce_scatter x1, waiting for transfers between devices, shards(): lax.psum_scatter(term_out, 'dp', scatter_dimension=0, tiled=True)  66.9 us
    unnamed x29, local copies, waits for them, and re-layouts  43.3 us
    another operation x1, local copies, waits for them, and re-layouts, shards(): jnp.stack([token_sum(query_rows, normed), token_sum(key_back, normed), to...  18.4 us
  transfers between devices with their start and end apart: 11, of which 11 were waited for; matrix products, arithmetic and copies ran while one was open for 12% of the time, Pallas kernels for 0%

commit v1 on v0

v1 whole, which is shorter than its diff:
```python
import math

import jax
import jax.numpy as jnp
from jax import lax
from jax.experimental import pallas as pl
from jax.experimental.pallas import tpu as pltpu
from jax.sharding import PartitionSpec as P

HEAD_DIM = 64
EPSILON = 1e-06
MASKED = -1e30
F32 = jnp.float32
BF16 = jnp.bfloat16
MESH = pl.DeviceIdType.MESH
QUERY_BLOCK = 256


def position_code(places, feature_width):
    half = feature_width // 2
    freqs = jnp.exp(jnp.arange(half, dtype=jnp.float32) * (-math.log(10000.0) / half))
    angle = places.astype(jnp.float32)[:, None] * freqs[None, :]
    return jnp.concatenate([jnp.sin(angle), jnp.cos(angle)], axis=1)


def layer_norm(inputs, places, ln_gain):
    shifted = inputs.astype(jnp.float32) + position_code(places, inputs.shape[1])
    centred = shifted - jnp.mean(shifted, axis=1, keepdims=True)
    inv_std = lax.rsqrt(jnp.mean(centred * centred, axis=1, keepdims=True) + EPSILON)
    standard = centred * inv_std
    normed = (standard * ln_gain).astype(jnp.bfloat16)
    return (normed, standard, inv_std)


def dot(left, right, left_dim, right_dim):
    return lax.dot_general(
        left, right, (((left_dim,), (right_dim,)), ((), ())), preferred_element_type=F32
    )


def turned(block):
    return block.astype(F32).T.astype(BF16)


def block_kernel(
    factor,
    normed_ref,
    masked_ref,
    standard_ref,
    inv_ref,
    gain_ref,
    bias_ref,
    w_qkv_ref,
    w_out_ref,
    d_tokens_ref,
    sums_ref,
    all_normed,
    all_masked,
    normed_t,
    masked_t,
    weights,
    out_weights,
    query,
    key,
    value,
    grad,
    query_t,
    key_grad_t,
    value_grad_t,
    grads,
    attended,
    returned,
    relayed,
    pieces,
    pieces_in,
    half_out,
    half_in,
    total,
    load_sem,
    gather_send,
    gather_recv,
    back_send,
    back_recv,
    sum_send,
    sum_recv,
):
    me = lax.axis_index("seq")
    place = lax.axis_index("dp")
    chip, core = me // 2, me % 2
    ahead, behind, across = (chip + 1) % 4, (chip + 3) % 4, (chip + 2) % 4
    twin = 1 - core
    after, before, far, mate = (
        ahead * 2 + core,
        behind * 2 + core,
        across * 2 + core,
        chip * 2 + twin,
    )
    after_twin, before_twin, far_twin = ahead * 2 + twin, behind * 2 + twin, across * 2 + twin
    layer, spot = place // 16, place % 16

    loads = [
        pltpu.make_async_copy(w_qkv_ref, weights, load_sem.at[0]),
        pltpu.make_async_copy(
            w_out_ref.at[:, pl.ds(pl.multiple_of(me * 128, 128), 128)], out_weights, load_sem.at[1]
        ),
        pltpu.make_async_copy(masked_ref, all_masked.at[me], load_sem.at[2]),
        pltpu.make_async_copy(normed_ref, all_normed.at[me], load_sem.at[3]),
    ]
    for load in loads:
        load.start()

    barrier = pltpu.get_barrier_semaphore()
    for step in range(1, 8):
        pl.semaphore_signal(
            barrier, inc=1, device_id={"seq": (me + step) % 8}, device_id_type=MESH
        )
    for step in range(1, 16):
        pl.semaphore_signal(
            barrier, inc=1, device_id={"dp": layer * 16 + (spot + step) % 16}, device_id_type=MESH
        )
    other_layer = (1 - layer) * 16 + spot
    pl.semaphore_signal(barrier, inc=1, device_id={"dp": other_layer}, device_id_type=MESH)
    pl.semaphore_wait(barrier, 23)

    def gather(index, source, target, device):
        return pltpu.make_async_remote_copy(
            src_ref=source,
            dst_ref=target,
            send_sem=gather_send.at[index],
            recv_sem=gather_recv.at[index],
            device_id={"seq": device},
            device_id_type=MESH,
        )

    started = []

    def go(copy):
        copy.start()
        started.append(copy)

    for base, own, full in ((0, masked_ref, all_masked), (13, normed_ref, all_normed)):
        go(gather(base + 0, own.at[0], full.at[me, 0], after))
        go(gather(base + 1, own.at[1], full.at[me, 1], before))
        go(gather(base + 2, own.at[1], full.at[me, 1], after))
        go(gather(base + 3, own.at[0], full.at[me, 0], before))
        go(gather(base + 4, own, full.at[me], mate))

    def landed(index, full, *spot_):
        view = full.at[spot_]
        gather(index, view, view, mate).wait_recv()

    def relay_near(base, full):
        landed(base + 0, full, before, 0)
        go(gather(base + 5, full.at[before, 0], full.at[before, 0], after))
        go(gather(base + 7, full.at[before, 0], full.at[before, 0], mate))
        landed(base + 1, full, after, 1)
        go(gather(base + 6, full.at[after, 1], full.at[after, 1], before))
        go(gather(base + 8, full.at[after, 1], full.at[after, 1], mate))
        landed(base + 2, full, before, 1)
        go(gather(base + 9, full.at[before, 1], full.at[before, 1], mate))
        landed(base + 3, full, after, 0)
        go(gather(base + 10, full.at[after, 0], full.at[after, 0], mate))

    def relay_far(base, full):
        landed(base + 5, full, far, 0)
        go(gather(base + 11, full.at[far, 0], full.at[far, 0], mate))
        landed(base + 6, full, far, 1)
        go(gather(base + 12, full.at[far, 1], full.at[far, 1], mate))

    def near_twin(base, full):
        landed(base + 4, full, mate)
        landed(base + 7, full, before_twin, 0)
        landed(base + 8, full, after_twin, 1)
        landed(base + 9, full, before_twin, 1)
        landed(base + 10, full, after_twin, 0)

    def far_twin_(base, full):
        landed(base + 11, full, far_twin, 0)
        landed(base + 12, full, far_twin, 1)

    def rows_of(which):
        return pl.ds(pl.multiple_of(which * 256, 256), 256)

    def project_masked(which):
        rows = rows_of(which)
        block = all_masked[pl.ds(which * 2, 2)].reshape(256, 1024)
        grad[rows, :] = dot(block, out_weights[...], 1, 0).astype(BF16)
        masked_t[:, rows] = turned(block)

    def project_normed(which):
        rows = rows_of(which)
        block = all_normed[pl.ds(which * 2, 2)].reshape(256, 1024)
        heads = pl.ds(pl.multiple_of(me * 128, 128), 128)
        queries = dot(block, weights[0, heads, :], 1, 1).astype(BF16).astype(F32) * 0.125
        query[rows, :] = queries.astype(BF16)
        query_t[:, rows] = queries.T.astype(BF16)
        key[rows, :] = dot(block, weights[1, heads, :], 1, 1).astype(BF16)
        value[rows, :] = dot(block, weights[2, heads, :], 1, 1).astype(BF16)
        normed_t[:, rows] = turned(block)

    for load in loads:
        load.wait()
    relay_near(0, all_masked)
    near_twin(0, all_masked)

    def near_masked(step, carry):
        project_masked((chip + 3 + step) % 4)
        return carry

    lax.fori_loop(0, 3, near_masked, 0)
    relay_near(13, all_normed)
    near_twin(13, all_normed)

    def near_normed(step, carry):
        project_normed((chip + 3 + step) % 4)
        return carry

    lax.fori_loop(0, 3, near_normed, 0)
    relay_far(0, all_masked)
    far_twin_(0, all_masked)
    project_masked(across)
    relay_far(13, all_normed)
    far_twin_(13, all_normed)
    project_normed(across)

    key_grad_t[...] = jnp.zeros_like(key_grad_t)
    value_grad_t[...] = jnp.zeros_like(value_grad_t)

    def attend(step, carry):
        rows = pl.ds(pl.multiple_of(step * QUERY_BLOCK, QUERY_BLOCK), QUERY_BLOCK)
        bias = bias_ref[...]
        for head in range(2):
            span = slice(head * HEAD_DIM, (head + 1) * HEAD_DIM)
            scores = dot(query[rows, span], key[:, span], 1, 1) + bias
            peak = jnp.max(scores, axis=1, keepdims=True)
            expo = jnp.exp(scores - peak)
            share = 1.0 / jnp.sum(expo, axis=1, keepdims=True)
            expo_low = expo.astype(BF16)
            mixed = dot(expo_low, value[:, span], 1, 0) * share
            scaled = grad[rows, span].astype(F32) * share
            delta = jnp.sum(mixed * scaled, axis=1, keepdims=True)
            prob_grad = dot(scaled.astype(BF16), value[:, span], 1, 1)
            score_grad = (expo * (prob_grad - delta)).astype(BF16)
            attended[rows, span] = mixed.astype(BF16)
            grads[rows, span] = (dot(score_grad, key[:, span], 1, 0) * 0.125).astype(BF16)
            key_grad_t[span, :] += dot(query_t[span, rows], score_grad, 1, 0)
            value_grad_t[span, :] += dot(scaled.T.astype(BF16), expo_low, 1, 0)
        return carry

    lax.fori_loop(0, 1024 // QUERY_BLOCK, attend, 0)
    grads[:, 128:256] = key_grad_t[...].T.astype(BF16)
    grads[:, 256:384] = value_grad_t[...].T.astype(BF16)

    def back(index, source, target, device):
        return pltpu.make_async_remote_copy(
            src_ref=source,
            dst_ref=target,
            send_sem=back_send.at[index],
            recv_sem=back_recv.at[index],
            device_id={"seq": device},
            device_id_type=MESH,
        )

    def slots(which):
        return grads.at[pl.ds(pl.multiple_of(which * 128, 128), 128), :]

    go(back(0, slots(far), relayed.at[0], after))
    go(back(1, slots(far_twin), relayed.at[1], before))
    go(back(2, slots(after), returned.at[me], after))
    go(back(3, slots(after_twin), returned.at[me], after_twin))
    go(back(4, slots(before), returned.at[me], before))
    go(back(5, slots(before_twin), returned.at[me], before_twin))
    go(back(6, slots(mate), returned.at[me], mate))

    pieces[:, :, :, :384] = dot(normed_t[...], grads[...], 1, 0).astype(BF16).reshape(2, 16, 32, 384)
    pieces[:, :, :, 384:] = (
        dot(masked_t[...], attended[...], 1, 0).astype(BF16).reshape(2, 16, 32, 128)
    )

    def scatter(step, source, target, device):
        return pltpu.make_async_remote_copy(
            src_ref=source,
            dst_ref=target,
            send_sem=sum_send.at[step],
            recv_sem=sum_recv.at[step],
            device_id={"dp": device},
            device_id_type=MESH,
        )

    for step in range(1, 16):
        to = (spot + step) % 16
        go(scatter(step, pieces.at[:, to], pieces_in.at[spot], layer * 16 + to))

    back(0, relayed.at[0], relayed.at[0], mate).wait_recv()
    go(back(7, relayed.at[0], returned.at[before], after))
    back(1, relayed.at[1], relayed.at[1], mate).wait_recv()
    go(back(8, relayed.at[1], returned.at[after], before_twin))

    def add_rows(which, block, first=False):
        heads = pl.ds(pl.multiple_of(which * 128, 128), 128)
        term = dot(block[:, :128], weights[0, heads, :], 1, 0)
        term = term + dot(block[:, 128:256], weights[1, heads, :], 1, 0)
        term = term + dot(block[:, 256:], weights[2, heads, :], 1, 0)
        total[...] = term if first else total[...] + term

    def came(index, which):
        back(index, returned.at[which], returned.at[which], mate).wait_recv()
        add_rows(which, returned[which])

    add_rows(me, grads[pl.ds(pl.multiple_of(me * 128, 128), 128), :], True)
    came(6, mate)
    came(2, before)
    came(3, before_twin)
    came(4, after)
    came(5, after_twin)

    for step in range(1, 16):
        view = pieces_in.at[(spot + 16 - step) % 16]
        scatter(step, view, view, other_layer).wait_recv()
    summed = pieces[:, spot].astype(F32)
    for step in range(1, 16):
        summed = summed + pieces_in[(spot + step) % 16].astype(F32)
    pieces_in[spot] = summed.astype(BF16)
    last = scatter(0, pieces_in.at[spot, 1 - layer], half_in, other_layer)
    go(last)

    came(7, far)
    came(8, far_twin)
    unit_grad = total[...] * gain_ref[...]
    standard = standard_ref[...]
    inner = unit_grad - jnp.mean(unit_grad, axis=1, keepdims=True)
    inner = inner - standard * jnp.mean(unit_grad * standard, axis=1, keepdims=True)
    own_masked = masked_ref[...].reshape(128, 1024).astype(F32)
    d_tokens_ref[...] = (own_masked + inv_ref[...] * inner).astype(BF16)

    last.wait_recv()
    half = jnp.where(layer == 0, summed[0], summed[1])
    sums_ref[...] = (half + half_in[...].astype(F32)) * factor
    for copy in started:
        copy.wait_send()


def shards(tokens, positions, counts, ln_gain, w_qkv, w_out, d_out):
    inputs = tokens[0]
    upstream = d_out[0]
    capacity, feature_width = inputs.shape
    shard_total = lax.axis_size("seq")
    shard_index = lax.axis_index("seq")
    slot_count = capacity * shard_total
    key_valid = jnp.arange(slot_count, dtype=jnp.int32) % capacity < jnp.repeat(counts[0], capacity)
    own_valid = lax.dynamic_slice_in_dim(key_valid, shard_index * capacity, capacity)
    normed, standard, inv_std = layer_norm(inputs, positions[0], ln_gain)
    masked = jnp.where(own_valid[:, None], upstream, jnp.zeros_like(upstream))
    bias = jnp.where(key_valid, 0.0, MASKED).astype(F32)[None, :]
    factor = 1.0 / math.sqrt(lax.axis_size("dp") * (3 * slot_count // 4))
    vmem = pl.BlockSpec(memory_space=pltpu.VMEM)
    anywhere = pl.BlockSpec(memory_space=pl.ANY)
    d_tokens, sums = pl.pallas_call(
        lambda *refs: block_kernel(factor, *refs),
        out_shape=(
            jax.ShapeDtypeStruct((128, 1024), BF16),
            jax.ShapeDtypeStruct((32, 512), F32),
        ),
        in_specs=[vmem] * 6 + [anywhere] * 2,
        out_specs=(vmem, vmem),
        scratch_shapes=[
            pltpu.VMEM((8, 2, 64, 1024), BF16),
            pltpu.VMEM((8, 2, 64, 1024), BF16),
            pltpu.VMEM((1024, 1024), BF16),
            pltpu.VMEM((1024, 1024), BF16),
            pltpu.VMEM((3, 1024, 1024), BF16),
            pltpu.VMEM((1024, 128), BF16),
            pltpu.VMEM((1024, 128), BF16),
            pltpu.VMEM((1024, 128), BF16),
            pltpu.VMEM((1024, 128), BF16),
            pltpu.VMEM((1024, 128), BF16),
            pltpu.VMEM((128, 1024), BF16),
            pltpu.VMEM((128, 1024), F32),
            pltpu.VMEM((128, 1024), F32),
            pltpu.VMEM((1024, 384), BF16),
            pltpu.VMEM((1024, 128), BF16),
            pltpu.VMEM((8, 128, 384), BF16),
            pltpu.VMEM((2, 128, 384), BF16),
            pltpu.VMEM((2, 16, 32, 512), BF16),
            pltpu.VMEM((16, 2, 32, 512), BF16),
            pltpu.VMEM((32, 512), BF16),
            pltpu.VMEM((32, 512), BF16),
            pltpu.VMEM((128, 1024), F32),
            pltpu.SemaphoreType.DMA((4,)),
            pltpu.SemaphoreType.DMA((26,)),
            pltpu.SemaphoreType.DMA((26,)),
            pltpu.SemaphoreType.DMA((9,)),
            pltpu.SemaphoreType.DMA((9,)),
            pltpu.SemaphoreType.DMA((16,)),
            pltpu.SemaphoreType.DMA((16,)),
        ],
        compiler_params=pltpu.CompilerParams(
            collective_id=0, has_side_effects=True, vmem_limit_bytes=60 * 1024 * 1024
        ),
        name="attention_block_grads",
    )(
        normed.reshape(2, 64, 1024),
        masked.reshape(2, 64, 1024),
        standard,
        inv_std,
        ln_gain[None, :],
        bias,
        w_qkv,
        w_out,
    )
    grad_qkv = jnp.transpose(sums[:, :384].reshape(32, 3, 128), (1, 2, 0))
    return (d_tokens[None], grad_qkv, sums[:, 384:])


def solution(mesh):
    placed = (
        P("dp", "seq", None),
        P("dp", "seq"),
        P("dp", None),
        P(),
        P(),
        P(),
        P("dp", "seq", None),
    )
    return jax.shard_map(
        shards,
        mesh=mesh,
        in_specs=placed,
        out_specs=(P("dp", "seq", None), P(None, "seq", "dp"), P("dp", "seq")),
        check_vma=False,
    )
```

time: 792 us -> 102 us (0.13)
  waiting for transfers between devices: 574 us -> 0 us
  Pallas kernels: 0 us -> 81.9 us
  local copies, waits for them, and re-layouts: 81.7 us -> 6.31 us
  starting transfers between devices: 44.1 us -> 0 us
  matrix products: 40.6 us -> 0 us
  between operations: 14.7 us -> 0.67 us
  blocking collectives: 14 us -> 0 us
    unnamed x6 -> x0, waiting for transfers between devices: 456 us -> none
    pallas_call x0 -> x1, Pallas kernels: none -> 81.9 us  [shards(): pl.pallas_call(lambda *refs: block_kernel(factor, *refs), out_shape=(jax....]
    reduce_scatter x2 -> x0, waiting for transfers between devices: 70.1 us -> none  [the longest x1 66.9 us: shards(): lax.psum_scatter(term_out, 'dp', scatter_dimension=0, tiled=True)]
    all_to_all x7 -> x0, waiting for transfers between devices: 48.5 us -> none  [the longest x1 10.7 us: shards(): lax.all_to_all(query_grad, 'seq', split_axis=0, concat_axis=1, tiled=True)]
    all_to_all x7 -> x0, starting transfers between devices: 44 us -> none  [the longest x1 9.94 us: shards(): lax.all_to_all(attn_grad, 'seq', split_axis=1, concat_axis=0, tiled=True)]
    unnamed x29 -> x2, local copies, waits for them, and re-layouts: 43.3 us -> 2.29 us
    dot_general x21 -> x0, matrix products: 33.9 us -> none  [the longest x4 9.81 us: token_sum(): lax.dot_general(left, right, (((0,), (0,)), ((), ())), preferred_element_...]
    another operation x1 -> x0, local copies, waits for them, and re-layouts: 18.4 us -> none  [shards(): jnp.stack([token_sum(query_rows, normed), token_sum(key_back, normed), to...]
  transfers between devices with their start and end apart: 11 -> 0, of which waited for: 11 -> 0; matrix products, arithmetic and copies ran while one was open for 12% -> 0% of each run, Pallas kernels for 0% -> 0%
where the time goes in v1:
time: 102 us; the launch traced here: 101 us
  Pallas kernels  81.9 us (80%)
  other arithmetic  12.3 us (12%)
  local copies, waits for them, and re-layouts  6.31 us (6%)
    pallas_call x1, Pallas kernels, shards(): pl.pallas_call(lambda *refs: block_kernel(factor, *refs), out_shape=(jax....  81.9 us
    unnamed x2, local copies, waits for them, and re-layouts  2.29 us

profile of v1, /device:TPU:1, one launch (start us, length us, event | category | flops | bytes accessed | tf_op | source)
XLA Modules:
  0.0 101.2 jit_solution(2166728191394814958)
XLA Ops:
  0.6 0.7 convert_bitcast_fusion
  1.3 1.0 multiply_sine_fusion
  2.3 1.1 %fusion.4 = f32[128]{0:T(128)S(1)} fusion(f32[128,512]{1,0:T(8,128)S(1)} %get-tuple-element.13, f32[128,512]{1,0:T(8,128)S(1)} %get-tuple-element.12, bf16[1,128,1024]{2,1,0:T(8,128)(2,1)} %param.7), kind=kLoop, calls=%fused_computation.15 | loop fusion | flops 524160 | bytes 786944 | tf_op jit(solution)/shard_map/reduce_sum | solution.py:28
  3.4 1.1 %multiply_reduce_fusion = f32[128]{0:T(128)S(1)} fusion(f32[128]{0:T(128)S(1)} %broadcast_multiply_fusion, f32[128,512]{1,0:T(8,128)S(1)} %get-tuple-element.13, f32[128,512]{1,0:T(8,128)S(1)} %get-tuple-element.12, bf16[1,128,1024]{2,1,0:T(8,128)(2,1)} %param.7), kind=kLoop, calls=%fused_computation.6 | loop fusion | flops 786304 | bytes 787456 | tf_op jit(solution)/shard_map/reduce_sum | solution.py:29
  4.5 1.9 %subtract_multiply_fusion.refs_2_ = f32[128,1024]{1,0:T(8,128)} fusion(f32[128]{0:T(128)S(1)} %get-tuple-element.15, f32[128]{0:T(128)S(1)} %broadcast_multiply_fusion, f32[128,512]{1,0:T(8,128)S(1)} %get-tuple-element.13, f32[128,512]{1,0:T(8,128)S(1)} %get-tuple-element.12, bf16[1,128,1024]{2,1,0:T(8,128)(2,1)} %param.7), kind=kLoop, calls=%fused_computation.7 | loop fusion | flops 655360 | bytes 1311744 | tf_op jit(solution)/shard_map/mul | solution.py:30
  6.4 0.1 rsqrt.8
  6.5 0.1 div.9
  6.6 0.7 convert_reduce_fusion
  7.3 0.1 convert_element_type.33
  7.3 1.0 multiply_sine_fusion.1
  8.3 1.8 %fusion.3.refs_0_ = bf16[2,64,1024]{2,1,0:T(8,128)(2,1)} fusion(f32[2,64,512]{2,1,0:T(8,128)S(1)} %get-tuple-element.11, f32[2,64,512]{2,1,0:T(8,128)S(1)} %get-tuple-element.10, f32[1024]{0:T(1024)} %param.10, f32[2,64]{1,0:T(2,128)S(1)} %rsqrt.8, f32[2,64]{1,0:T(2,128)S(1)} %div.9, bf16[2,64,1024]{2,1,0:T(8,128)(2,1)} %bitcast.22), kind=kLoop, calls=%fused_computation.4 | loop fusion | flops 917504 | bytes 1053696 | tf_op jit(solution)/shard_map/convert_element_type | solution.py:31
  10.1 0.7 copy.12.refs_3_
  10.9 0.7 fusion.5
  11.6 0.1 dynamic_slice.3
  11.7 0.1 broadcast_in_dim.38
  11.8 1.7 %broadcast_select_fusion.refs_1_ = bf16[2,64,1024]{2,1,0:T(8,128)(2,1)} fusion(bf16[2,64,1024]{2,1,0:T(8,128)(2,1)} %bitcast.23, pred[2,64]{1,0:T(4,128)(4,1)S(1)} %broadcast_in_dim.38), kind=kLoop, calls=%fused_computation.12 | loop fusion | flops 131072 | bytes 524416 | tf_op jit(solution)/shard_map/jit(_where)/select_n | solution.py:353
  13.5 0.7 broadcast_in_dim.37
  14.2 0.6 compare_select_fusion.refs_5_
  14.8 81.9 %attention_block_grads.1 = (bf16[128,1024]{1,0:T(8,128)(2,1)}, f32[32,512]{1,0:T(8,128)}) custom-call(bf16[2,64,1024]{2,1,0:T(8,128)(2,1)} %fusion.3.refs_0_, bf16[2,64,1024]{2,1,0:T(8,128)(2,1)} %broadcast_select_fusion.refs_1_, f32[128,1024]{1,0:T(8,128)} %subtract_multiply_fusion.refs_2_, f32[128,1]{1,0:T(8,128)} %copy.12.refs_3_, f32[1,1024]{1,0:T(1,128)} %bitcast.26, ...), custom_call_target="tpu_custom_call" | custom-call | tf_op jit(solution)/shard_map/attention_block_grads/pallas_call | solution.py:358
  96.8 0.8 slice.6
  97.6 0.6 copy.13
  98.2 1.3 %slice.7 = f32[32,128]{1,0:T(8,128)} slice(f32[32,512]{1,0:T(8,128)} %get-tuple-element.6), slice={[0:32], [384:512]} | slice | bytes 32768 | tf_op jit(solution)/shard_map/slice | solution.py:412
  99.5 1.7 %copy.15 = bf16[1,128,1024]{2,1,0:T(8,128)(2,1)} copy(bf16[1,128,1024]{2,1,0:T(8,128)(2,1)} %bitcast.25) | data formatting | bytes 524288
  (4 shorter events, 0.0 us)

commit v2 on v1

v2 whole, which is shorter than its diff:
```python
import math

import jax
import jax.numpy as jnp
from jax import lax
from jax.experimental import pallas as pl
from jax.experimental.pallas import tpu as pltpu
from jax.sharding import PartitionSpec as P

HEAD_DIM = 64
EPSILON = 1e-06
MASKED = -1e30
F32 = jnp.float32
BF16 = jnp.bfloat16
MESH = pl.DeviceIdType.MESH
QUERY_BLOCK = 256


def sin_cos(angle):
    turns = jnp.floor(angle * (2.0 / math.pi) + 0.5)
    rest = angle - turns * 1.5703125
    rest = rest - turns * 4.837512969970703125e-4
    rest = rest - turns * 7.54978995489188216e-8
    square = rest * rest
    sine = rest + rest * square * (
        -1.6666654611e-1 + square * (8.3321608736e-3 - square * 1.9515295891e-4)
    )
    cosine = (
        1.0
        - 0.5 * square
        + square
        * square
        * (4.166664568298827e-2 + square * (-1.388731625493765e-3 + square * 2.443315711809948e-5))
    )
    quarter = turns - 4.0 * jnp.floor(turns * 0.25)
    odd = (quarter == 1.0) | (quarter == 3.0)
    sine, cosine = jnp.where(odd, cosine, sine), jnp.where(odd, sine, cosine)
    sine = jnp.where(quarter >= 2.0, -sine, sine)
    cosine = jnp.where((quarter == 1.0) | (quarter == 2.0), -cosine, cosine)
    return sine, cosine


def dot(left, right, left_dim, right_dim):
    return lax.dot_general(
        left, right, (((left_dim,), (right_dim,)), ((), ())), preferred_element_type=F32
    )


def turned(block):
    return block.astype(F32).T.astype(BF16)


def block_kernel(
    factor,
    tokens_ref,
    d_out_ref,
    positions_ref,
    counts_ref,
    gain_ref,
    w_qkv_ref,
    w_out_ref,
    d_tokens_ref,
    sums_ref,
    normed_ref,
    masked_ref,
    standard_ref,
    inv_ref,
    bias_ref,
    expos,
    mixes,
    shares,
    all_normed,
    all_masked,
    normed_t,
    masked_t,
    weights,
    out_weights,
    query,
    key,
    value,
    grad,
    query_t,
    key_grad_t,
    value_grad_t,
    grads,
    attended,
    returned,
    relayed,
    out_part,
    pieces,
    row_in,
    column_in,
    row_low,
    column_low,
    row_end,
    column_end,
    out_pieces,
    out_pieces_in,
    half_out,
    half_in,
    total,
    load_sem,
    gather_send,
    gather_recv,
    back_send,
    back_recv,
    sum_send,
    sum_recv,
):
    me = lax.axis_index("seq")
    place = lax.axis_index("dp")
    chip, core = me // 2, me % 2
    ahead, behind, across = (chip + 1) % 4, (chip + 3) % 4, (chip + 2) % 4
    twin = 1 - core
    after, before, far, mate = (
        ahead * 2 + core,
        behind * 2 + core,
        across * 2 + core,
        chip * 2 + twin,
    )
    after_twin, before_twin, far_twin = ahead * 2 + twin, behind * 2 + twin, across * 2 + twin
    layer, spot = place // 16, place % 16

    loads = [
        pltpu.make_async_copy(w_qkv_ref, weights, load_sem.at[0]),
        pltpu.make_async_copy(
            w_out_ref.at[:, pl.ds(pl.multiple_of(me * 128, 128), 128)], out_weights, load_sem.at[1]
        ),
    ]
    for load in loads:
        load.start()

    barrier = pltpu.get_barrier_semaphore()
    for step in range(1, 8):
        pl.semaphore_signal(
            barrier, inc=1, device_id={"seq": (me + step) % 8}, device_id_type=MESH
        )
    for step in range(1, 16):
        pl.semaphore_signal(
            barrier, inc=1, device_id={"dp": layer * 16 + (spot + step) % 16}, device_id_type=MESH
        )
    other_layer = (1 - layer) * 16 + spot
    pl.semaphore_signal(barrier, inc=1, device_id={"dp": other_layer}, device_id_type=MESH)

    slot = lax.broadcasted_iota(jnp.int32, (1, 128), 1)
    for part in range(8):
        bias_ref[:, part * 128 : (part + 1) * 128] = jnp.where(
            slot < counts_ref[0, part], 0.0, MASKED
        )
    row = lax.broadcasted_iota(jnp.int32, (128, 128), 0)
    lane = lax.broadcasted_iota(jnp.int32, (128, 128), 1)
    places = jnp.sum(
        jnp.where(row == lane, positions_ref[...].astype(F32), 0.0), axis=1, keepdims=True
    )
    freqs = jnp.exp(
        lax.broadcasted_iota(jnp.int32, (1, 512), 1).astype(F32) * (-math.log(10000.0) / 512)
    )
    own_count = counts_ref[0, me]
    for part in range(4):
        rows = slice(part * 32, (part + 1) * 32)
        sine, cosine = sin_cos(places[rows] * freqs)
        shifted = tokens_ref[rows, :].astype(F32) + jnp.concatenate([sine, cosine], axis=1)
        centred = shifted - jnp.mean(shifted, axis=1, keepdims=True)
        inv_std = lax.rsqrt(jnp.mean(centred * centred, axis=1, keepdims=True) + EPSILON)
        unit = centred * inv_std
        standard_ref[rows, :] = unit
        inv_ref[rows, :] = inv_std
        within = slice((part % 2) * 32, (part % 2) * 32 + 32)
        normed_ref[part // 2, within, :] = (unit * gain_ref[...]).astype(BF16)
        upstream = d_out_ref[rows, :]
        spots = lax.broadcasted_iota(jnp.int32, (32, 1024), 0) + part * 32
        masked_ref[part // 2, within, :] = jnp.where(
            spots < own_count, upstream.astype(F32), 0.0
        ).astype(BF16)
    all_normed[me] = normed_ref[...]
    all_masked[me] = masked_ref[...]
    pl.semaphore_wait(barrier, 23)

    def gather(index, source, target, device):
        return pltpu.make_async_remote_copy(
            src_ref=source,
            dst_ref=target,
            send_sem=gather_send.at[index],
            recv_sem=gather_recv.at[index],
            device_id={"seq": device},
            device_id_type=MESH,
        )

    started = []

    def go(copy):
        copy.start()
        started.append(copy)

    def send_own(base, own, full):
        go(gather(base + 0, own.at[0], full.at[me, 0], after))
        go(gather(base + 1, own.at[1], full.at[me, 1], before))
        go(gather(base + 2, own.at[1], full.at[me, 1], after))
        go(gather(base + 3, own.at[0], full.at[me, 0], before))
        go(gather(base + 4, own, full.at[me], mate))

    def landed(index, full, *spot_):
        view = full.at[spot_]
        gather(index, view, view, mate).wait_recv()

    def relay_first(base, full):
        landed(base + 0, full, before, 0)
        go(gather(base + 5, full.at[before, 0], full.at[before, 0], after))
        go(gather(base + 7, full.at[before, 0], full.at[before, 0], mate))
        landed(base + 1, full, after, 1)
        go(gather(base + 6, full.at[after, 1], full.at[after, 1], before))
        go(gather(base + 8, full.at[after, 1], full.at[after, 1], mate))

    def relay_second(base, full):
        landed(base + 2, full, before, 1)
        go(gather(base + 9, full.at[before, 1], full.at[before, 1], mate))
        landed(base + 3, full, after, 0)
        go(gather(base + 10, full.at[after, 0], full.at[after, 0], mate))

    def relay_far(base, full):
        landed(base + 5, full, far, 0)
        go(gather(base + 11, full.at[far, 0], full.at[far, 0], mate))
        landed(base + 6, full, far, 1)
        go(gather(base + 12, full.at[far, 1], full.at[far, 1], mate))

    upper, lower = slice(0, 32), slice(32, 64)

    def relay_first_fine(base, full):
        landed(base + 0, full, before, 0)
        go(gather(base + 5, full.at[before, 0, upper], full.at[before, 0, upper], after))
        go(gather(26, full.at[before, 0, lower], full.at[before, 0, lower], after))
        go(gather(base + 7, full.at[before, 0], full.at[before, 0], mate))
        landed(base + 1, full, after, 1)
        go(gather(base + 6, full.at[after, 1, upper], full.at[after, 1, upper], before))
        go(gather(27, full.at[after, 1, lower], full.at[after, 1, lower], before))
        go(gather(base + 8, full.at[after, 1], full.at[after, 1], mate))

    def relay_far_fine(base, full):
        landed(base + 5, full, far, 0, upper)
        go(gather(base + 11, full.at[far, 0, upper], full.at[far, 0, upper], mate))
        landed(base + 6, full, far, 1, upper)
        go(gather(base + 12, full.at[far, 1, upper], full.at[far, 1, upper], mate))
        landed(26, full, far, 0, lower)
        go(gather(28, full.at[far, 0, lower], full.at[far, 0, lower], mate))
        landed(27, full, far, 1, lower)
        go(gather(29, full.at[far, 1, lower], full.at[far, 1, lower], mate))

    def far_twin_fine(base, full):
        landed(base + 11, full, far_twin, 0, upper)
        landed(base + 12, full, far_twin, 1, upper)
        landed(28, full, far_twin, 0, lower)
        landed(29, full, far_twin, 1, lower)

    def near_twin(base, full):
        landed(base + 4, full, mate)
        landed(base + 7, full, before_twin, 0)
        landed(base + 8, full, after_twin, 1)
        landed(base + 9, full, before_twin, 1)
        landed(base + 10, full, after_twin, 0)

    def far_twin_(base, full):
        landed(base + 11, full, far_twin, 0)
        landed(base + 12, full, far_twin, 1)

    def rows_of(which):
        return pl.ds(pl.multiple_of(which * 256, 256), 256)

    def project_masked(which):
        rows = rows_of(which)
        block = all_masked[pl.ds(which * 2, 2)].reshape(256, 1024)
        grad[rows, :] = dot(block, out_weights[...], 1, 0).astype(BF16)

    def add_out_terms(which):
        rows = rows_of(which)
        block = all_masked[pl.ds(which * 2, 2)].reshape(256, 1024)
        masked_t[...] = turned(block)
        out_part[...] += dot(masked_t[...], attended[rows, :], 1, 0)

    def project_normed(which):
        rows = rows_of(which)
        block = all_normed[pl.ds(which * 2, 2)].reshape(256, 1024)
        heads = pl.ds(pl.multiple_of(me * 128, 128), 128)
        queries = dot(block, weights[0, heads, :], 1, 1).astype(BF16).astype(F32) * 0.125
        query[rows, :] = queries.astype(BF16)
        query_t[:, rows] = queries.T.astype(BF16)
        key[rows, :] = dot(block, weights[1, heads, :], 1, 1).astype(BF16)
        value[rows, :] = dot(block, weights[2, heads, :], 1, 1).astype(BF16)
        normed_t[:, rows] = turned(block)

    def mix(step, carry):
        rows = pl.ds(pl.multiple_of(step * QUERY_BLOCK, QUERY_BLOCK), QUERY_BLOCK)
        bias = bias_ref[...]
        for head in range(2):
            span = slice(head * HEAD_DIM, (head + 1) * HEAD_DIM)
            scores = dot(query[rows, span], key[:, span], 1, 1) + bias
            peak = jnp.max(scores, axis=1, keepdims=True)
            expo = jnp.exp(scores - peak)
            expos[head, rows, :] = expo
            share = 1.0 / jnp.sum(expo, axis=1, keepdims=True)
            mixed = dot(expo.astype(BF16), value[:, span], 1, 0) * share
            mixes[rows, span] = mixed
            shares[rows, span] = jnp.broadcast_to(share, (QUERY_BLOCK, HEAD_DIM))
            attended[rows, span] = mixed.astype(BF16)
        return carry

    def attend(which):
        rows = rows_of(which)
        scaled = grad[rows, :].astype(F32) * shares[rows, :]
        scaled_low = scaled.astype(BF16)
        scaled_t = scaled.T.astype(BF16)
        products = mixes[rows, :] * scaled
        for head in range(2):
            span = slice(head * HEAD_DIM, (head + 1) * HEAD_DIM)
            delta = jnp.sum(products[:, span], axis=1, keepdims=True)
            expo = expos[head, rows, :]
            prob_grad = dot(scaled_low[:, span], value[:, span], 1, 1)
            score_grad = (expo * (prob_grad - delta)).astype(BF16)
            grads[rows, span] = (dot(score_grad, key[:, span], 1, 0) * 0.125).astype(BF16)
            key_grad_t[span, :] += dot(query_t[span, rows], score_grad, 1, 0)
            value_grad_t[span, :] += dot(scaled_t[span, :], expo.astype(BF16), 1, 0)

    def back(index, source, target, device):
        return pltpu.make_async_remote_copy(
            src_ref=source,
            dst_ref=target,
            send_sem=back_send.at[index],
            recv_sem=back_recv.at[index],
            device_id={"seq": device},
            device_id_type=MESH,
        )

    def slots(which, columns=slice(0, 384)):
        return grads.at[pl.ds(pl.multiple_of(which * 128, 128), 128), columns]

    first, rest = slice(0, 128), slice(128, 384)

    def send_queries(index, which):
        go(back(index, slots(which, first), returned.at[me, :, first], which))

    def send_rest(index, which):
        go(back(index, slots(which, rest), returned.at[me, :, rest], which))

    across_x, across_y = spot % 4, spot // 4

    def at(step_x, step_y):
        return ((across_y + step_y) % 4) * 4 + (across_x + step_x) % 4

    hops = [(x, y) for y in range(4) for x in range(4) if (x, y) != (0, 0)]

    def scatter(index, source, target, device):
        return pltpu.make_async_remote_copy(
            src_ref=source,
            dst_ref=target,
            send_sem=sum_send.at[index],
            recv_sem=sum_recv.at[index],
            device_id={"dp": device},
            device_id_type=MESH,
        )

    def exchange(base, source, target):
        for x, y in hops:
            to = at(x, y)
            go(scatter(base + y * 4 + x, source.at[:, to], target.at[spot], layer * 16 + to))

    def collect(base, target):
        for x, y in hops:
            view = target.at[at(4 - x, 4 - y)]
            scatter(base + y * 4 + x, view, view, other_layer).wait_recv()

    def add_pieces(own, target):
        summed = own[:, spot].astype(F32)
        for x, y in hops:
            summed = summed + target[at(x, y)].astype(F32)
        return summed

    send_own(0, normed_ref, all_normed)
    for load in loads:
        load.wait()
    out_part[...] = jnp.zeros_like(out_part)
    key_grad_t[...] = jnp.zeros_like(key_grad_t)
    value_grad_t[...] = jnp.zeros_like(value_grad_t)
    relay_first(0, all_normed)
    send_own(13, masked_ref, all_masked)
    relay_second(0, all_normed)
    near_twin(0, all_normed)

    def near_normed(step, carry):
        project_normed((chip + 3 + step) % 4)
        return carry

    lax.fori_loop(0, 3, near_normed, 0)
    relay_far(0, all_normed)
    far_twin_(0, all_normed)
    project_normed(across)
    lax.fori_loop(0, 1024 // QUERY_BLOCK, mix, 0)

    relay_first_fine(13, all_masked)
    relay_second(13, all_masked)
    near_twin(13, all_masked)

    def near_masked(step, carry):
        which = (chip + 3 + step) % 4
        project_masked(which)
        attend(which)
        add_out_terms(which)
        return carry

    lax.fori_loop(0, 3, near_masked, 0)
    send_queries(9, after)
    send_queries(10, after_twin)
    send_queries(11, before)
    send_queries(12, before_twin)
    send_queries(13, mate)
    relay_far_fine(13, all_masked)
    far_twin_fine(13, all_masked)
    project_masked(across)
    attend(across)
    grads[:, 128:256] = key_grad_t[...].T.astype(BF16)
    grads[:, 256:384] = value_grad_t[...].T.astype(BF16)

    go(back(0, slots(far), relayed.at[0], after))
    go(back(1, slots(far_twin), relayed.at[1], before))
    send_rest(2, after)
    send_rest(3, after_twin)
    send_rest(4, before)
    send_rest(5, before_twin)
    send_rest(6, mate)

    pieces[...] = dot(normed_t[...], grads[...], 1, 0).astype(BF16).reshape(2, 4, 4, 32, 384)
    for step in range(1, 4):
        to_x, to_y = (across_x + step) % 4, (across_y + step) % 4
        go(scatter(step, pieces.at[0, :, to_x], row_in.at[across_x], layer * 16 + at(step, 0)))
        go(scatter(step + 3, pieces.at[1, to_y], column_in.at[across_y], layer * 16 + at(0, step)))
    add_out_terms(across)
    out_pieces[...] = out_part[...].astype(BF16).reshape(2, 16, 32, 128)
    exchange(20, out_pieces, out_pieces_in)

    def add_rows(which, block, first=False):
        heads = pl.ds(pl.multiple_of(which * 128, 128), 128)
        term = dot(block[:, :128], weights[0, heads, :], 1, 0)
        term = term + dot(block[:, 128:256], weights[1, heads, :], 1, 0)
        term = term + dot(block[:, 256:], weights[2, heads, :], 1, 0)
        total[...] = term if first else total[...] + term

    def came(index, which, columns=rest):
        view = returned.at[which, :, columns]
        back(index, view, view, mate).wait_recv()

    def came_near(index, which):
        came(index + 7, which, first)
        came(index, which)
        add_rows(which, returned[which])

    add_rows(me, grads[pl.ds(pl.multiple_of(me * 128, 128), 128), :], True)
    came_near(6, mate)
    back(0, relayed.at[0], relayed.at[0], mate).wait_recv()
    go(back(7, relayed.at[0], returned.at[before], after))
    back(1, relayed.at[1], relayed.at[1], mate).wait_recv()
    go(back(8, relayed.at[1], returned.at[after], before_twin))
    row_sum = pieces[0, :, across_x].astype(F32)
    column_sum = pieces[1, across_y].astype(F32)
    for step in range(1, 4):
        from_x, from_y = (across_x + 4 - step) % 4, (across_y + 4 - step) % 4
        view = row_in.at[from_x]
        scatter(step, view, view, other_layer).wait_recv()
        row_sum = row_sum + row_in[from_x].astype(F32)
        view = column_in.at[from_y]
        scatter(step + 3, view, view, other_layer).wait_recv()
        column_sum = column_sum + column_in[from_y].astype(F32)
    row_low[...] = row_sum.astype(BF16)
    column_low[...] = column_sum.astype(BF16)
    for step in range(1, 4):
        to_x, to_y = (across_x + step) % 4, (across_y + step) % 4
        go(scatter(step + 6, row_low.at[to_y], row_end.at[across_y], layer * 16 + at(0, step)))
        go(scatter(step + 9, column_low.at[to_x], column_end.at[across_x], layer * 16 + at(step, 0)))
    came_near(2, before)
    came_near(3, before_twin)

    collect(20, out_pieces_in)
    out_summed = add_pieces(out_pieces, out_pieces_in)
    half_out[:, :, 384:] = out_summed.astype(BF16)
    row_total = row_low[across_y].astype(F32)
    column_total = column_low[across_x].astype(F32)
    for step in range(1, 4):
        from_x, from_y = (across_x + 4 - step) % 4, (across_y + 4 - step) % 4
        view = row_end.at[from_y]
        scatter(step + 6, view, view, other_layer).wait_recv()
        row_total = row_total + row_end[from_y].astype(F32)
        view = column_end.at[from_x]
        scatter(step + 9, view, view, other_layer).wait_recv()
        column_total = column_total + column_end[from_x].astype(F32)
    half_out[0, :, :384] = row_total.astype(BF16)
    half_out[1, :, :384] = column_total.astype(BF16)
    last = scatter(0, half_out.at[1 - layer], half_in, other_layer)
    go(last)
    came_near(4, after)
    came_near(5, after_twin)

    came(7, far, slice(0, 384))
    add_rows(far, returned[far])
    came(8, far_twin, slice(0, 384))
    add_rows(far_twin, returned[far_twin])
    unit_grad = total[...] * gain_ref[...]
    standard = standard_ref[...]
    inner = unit_grad - jnp.mean(unit_grad, axis=1, keepdims=True)
    inner = inner - standard * jnp.mean(unit_grad * standard, axis=1, keepdims=True)
    own_masked = masked_ref[...].reshape(128, 1024).astype(F32)
    d_tokens_ref[...] = (own_masked + inv_ref[...] * inner).astype(BF16)

    last.wait_recv()
    far_half = half_in[...].astype(F32)
    half = jnp.where(layer == 0, row_total, column_total)
    sums_ref[:, :384] = (half + far_half[:, :384]) * factor
    half = jnp.where(layer == 0, out_summed[0], out_summed[1])
    sums_ref[:, 384:] = (half + far_half[:, 384:]) * factor
    for copy in started:
        copy.wait_send()


def place_results(rows_ref, sums_ref, d_tokens_ref, grad_qkv_ref, grad_out_ref):
    d_tokens_ref[...] = rows_ref[...]
    for part in range(3):
        grad_qkv_ref[part] = sums_ref[:, part * 128 : (part + 1) * 128]
    grad_out_ref[...] = sums_ref[:, 384:]


def shards(tokens, positions, counts, ln_gain, w_qkv, w_out, d_out):
    slot_count = tokens.shape[1] * lax.axis_size("seq")
    factor = 1.0 / math.sqrt(lax.axis_size("dp") * (3 * slot_count // 4))
    vmem = pl.BlockSpec(memory_space=pltpu.VMEM)
    anywhere = pl.BlockSpec(memory_space=pl.ANY)
    rows, sums = pl.pallas_call(
        lambda *refs: block_kernel(factor, *refs),
        out_shape=(
            jax.ShapeDtypeStruct((128, 1024), BF16),
            jax.ShapeDtypeStruct((32, 512), F32),
        ),
        in_specs=[
            vmem,
            vmem,
            vmem,
            pl.BlockSpec(memory_space=pltpu.SMEM),
            vmem,
            anywhere,
            anywhere,
        ],
        out_specs=(vmem, vmem),
        scratch_shapes=[
            pltpu.VMEM((2, 64, 1024), BF16),
            pltpu.VMEM((2, 64, 1024), BF16),
            pltpu.VMEM((128, 1024), F32),
            pltpu.VMEM((128, 1), F32),
            pltpu.VMEM((1, 1024), F32),
            pltpu.VMEM((2, 1024, 1024), F32),
            pltpu.VMEM((1024, 128), F32),
            pltpu.VMEM((1024, 128), F32),
            pltpu.VMEM((8, 2, 64, 1024), BF16),
            pltpu.VMEM((8, 2, 64, 1024), BF16),
            pltpu.VMEM((1024, 1024), BF16),
            pltpu.VMEM((1024, 256), BF16),
            pltpu.VMEM((3, 1024, 1024), BF16),
            pltpu.VMEM((1024, 128), BF16),
            pltpu.VMEM((1024, 128), BF16),
            pltpu.VMEM((1024, 128), BF16),
            pltpu.VMEM((1024, 128), BF16),
            pltpu.VMEM((1024, 128), BF16),
            pltpu.VMEM((128, 1024), BF16),
            pltpu.VMEM((128, 1024), F32),
            pltpu.VMEM((128, 1024), F32),
            pltpu.VMEM((1024, 384), BF16),
            pltpu.VMEM((1024, 128), BF16),
            pltpu.VMEM((8, 128, 384), BF16),
            pltpu.VMEM((2, 128, 384), BF16),
            pltpu.VMEM((1024, 128), F32),
            pltpu.VMEM((2, 4, 4, 32, 384), BF16),
            pltpu.VMEM((4, 4, 32, 384), BF16),
            pltpu.VMEM((4, 4, 32, 384), BF16),
            pltpu.VMEM((4, 32, 384), BF16),
            pltpu.VMEM((4, 32, 384), BF16),
            pltpu.VMEM((4, 32, 384), BF16),
            pltpu.VMEM((4, 32, 384), BF16),
            pltpu.VMEM((2, 16, 32, 128), BF16),
            pltpu.VMEM((16, 2, 32, 128), BF16),
            pltpu.VMEM((2, 32, 512), BF16),
            pltpu.VMEM((32, 512), BF16),
            pltpu.VMEM((128, 1024), F32),
            pltpu.SemaphoreType.DMA((2,)),
            pltpu.SemaphoreType.DMA((30,)),
            pltpu.SemaphoreType.DMA((30,)),
            pltpu.SemaphoreType.DMA((14,)),
            pltpu.SemaphoreType.DMA((14,)),
            pltpu.SemaphoreType.DMA((36,)),
            pltpu.SemaphoreType.DMA((36,)),
        ],
        compiler_params=pltpu.CompilerParams(
            collective_id=0, has_side_effects=True, vmem_limit_bytes=60 * 1024 * 1024
        ),
        name="attention_block_grads",
    )(tokens[0], d_out[0], positions, counts, ln_gain[None, :], w_qkv, w_out)
    d_tokens, grad_qkv, grad_out = pl.pallas_call(
        place_results,
        out_shape=(
            jax.ShapeDtypeStruct((128, 1024), BF16),
            jax.ShapeDtypeStruct((3, 32, 128), F32),
            jax.ShapeDtypeStruct((32, 128), F32),
        ),
        in_specs=[vmem] * 2,
        out_specs=(vmem,) * 3,
        name="place_results",
    )(rows, sums)
    return (d_tokens[None], jnp.transpose(grad_qkv, (0, 2, 1)), grad_out)


def solution(mesh):
    placed = (
        P("dp", "seq", None),
        P("dp", "seq"),
        P("dp", None),
        P(),
        P(),
        P(),
        P("dp", "seq", None),
    )
    return jax.shard_map(
        shards,
        mesh=mesh,
        in_specs=placed,
        out_specs=(P("dp", "seq", None), P(None, "seq", "dp"), P("dp", "seq")),
        check_vma=False,
    )
```

time: 102 us -> 75.8 us (0.74)
  other arithmetic: 12.3 us -> 0 us
  Pallas kernels: 81.9 us -> 75.1 us
  local copies, waits for them, and re-layouts: 6.31 us -> 0 us
    pallas_call x1, Pallas kernels: 81.9 us -> 73.4 us  [shards(): pl.pallas_call(lambda *refs: block_kernel(factor, *refs), out_shape=(jax....]
    convert_element_type x3 -> x0, other arithmetic: 3.15 us -> none  [the longest x1 1.81 us: layer_norm(): normed = (standard * ln_gain).astype(jnp.bfloat16)]
    select_n x2 -> x0, other arithmetic: 2.34 us -> none  [the longest x1 1.74 us: shards(): masked = jnp.where(own_valid[:, None], upstream, jnp.zeros_like(upstream))]
    unnamed x2 -> x0, local copies, waits for them, and re-layouts: 2.29 us -> none
    reduce_sum x2 -> x0, other arithmetic: 2.24 us -> none  [the longest x1 1.15 us: layer_norm(): jnp.mean(centred * centred, axis=1, keepdims=True) + EPSILON]
    slice x2 -> x0, local copies, waits for them, and re-layouts: 2.13 us -> none  [the longest x1 1.32 us: shards(): return (d_tokens[None], grad_qkv, sums[:, 384:])]
    sin x2 -> x0, other arithmetic: 1.97 us -> none  [position_code(): return jnp.concatenate([jnp.sin(angle), jnp.cos(angle)], axis=1)]
    mul x1 -> x0, other arithmetic: 1.87 us -> none  [layer_norm(): standard = centred * inv_std]
where the time goes in v2:
time: 75.8 us; the launch traced here: 75.7 us
  Pallas kernels  75.1 us (99%)
    pallas_call x1, Pallas kernels, shards(): pl.pallas_call(lambda *refs: block_kernel(factor, *refs), out_shape=(jax....  73.4 us
    pallas_call x1, Pallas kernels, shards(): pl.pallas_call(place_results, out_shape=(jax.ShapeDtypeStruct((128, 1024)...  1.68 us

profile of v2, /device:TPU:1, one launch (start us, length us, event | category | flops | bytes accessed | tf_op | source)
XLA Modules:
  0.0 75.7 jit_solution(16048921067805837825)
XLA Ops:
  0.6 73.4 %attention_block_grads.1 = (bf16[128,1024]{1,0:T(8,128)(2,1)}, f32[32,512]{1,0:T(8,128)}) custom-call(bf16[128,1024]{1,0:T(8,128)(2,1)} %bitcast.5, bf16[128,1024]{1,0:T(8,128)(2,1)} %bitcast.6, s32[1,128]{1,0:T(1,128)} %refs_2_.1, s32[1,8]{1,0:T(1,128)} %refs_3_.1, f32[1,1024]{1,0:T(1,128)} %bitcast.7, bf16[3,1024,1024]{2,1,0:T(8,128)(2,1)} %refs_5_.1, ...), custom_call_target="tpu_custom_call" | custom-call | tf_op jit(solution)/shard_map/attention_block_grads/pallas_call | solution.py:532
  74.0 1.7 %place_results.1 = (bf16[128,1024]{1,0:T(8,128)(2,1)}, f32[3,32,128]{2,1,0:T(8,128)}, f32[32,128]{1,0:T(8,128)}) custom-call(bf16[128,1024]{1,0:T(8,128)(2,1)} %get-tuple-element.8.rows_ref, f32[32,512]{1,0:T(8,128)} %get-tuple-element.9.sums_ref), custom_call_target="tpu_custom_call" | custom-call | tf_op jit(solution)/shard_map/place_results/pallas_call | solution.py:600

commit v3 on v2

--- a/solution.py
+++ b/solution.py
@@ -52,8 +52,8 @@
 
 def block_kernel(
     factor,
-    tokens_ref,
-    d_out_ref,
+    tokens_hbm,
+    d_out_hbm,
     positions_ref,
     counts_ref,
     gain_ref,
@@ -61,6 +61,8 @@
     w_out_ref,
     d_tokens_ref,
     sums_ref,
+    tokens_ref,
+    d_out_ref,
     normed_ref,
     masked_ref,
     standard_ref,
@@ -121,15 +123,18 @@
     after_twin, before_twin, far_twin = ahead * 2 + twin, behind * 2 + twin, across * 2 + twin
     layer, spot = place // 16, place % 16
 
+    early = [
+        pltpu.make_async_copy(tokens_hbm, tokens_ref, load_sem.at[2]),
+        pltpu.make_async_copy(d_out_hbm, d_out_ref, load_sem.at[3]),
+    ]
+    for load in early:
+        load.start()
     loads = [
         pltpu.make_async_copy(w_qkv_ref, weights, load_sem.at[0]),
         pltpu.make_async_copy(
             w_out_ref.at[:, pl.ds(pl.multiple_of(me * 128, 128), 128)], out_weights, load_sem.at[1]
         ),
     ]
-    for load in loads:
-        load.start()
-
     barrier = pltpu.get_barrier_semaphore()
     for step in range(1, 8):
         pl.semaphore_signal(
@@ -156,6 +161,10 @@
         lax.broadcasted_iota(jnp.int32, (1, 512), 1).astype(F32) * (-math.log(10000.0) / 512)
     )
     own_count = counts_ref[0, me]
+    for load in early:
+        load.wait()
+    for load in loads:
+        load.start()
     for part in range(4):
         rows = slice(part * 32, (part + 1) * 32)
         sine, cosine = sin_cos(places[rows] * freqs)
@@ -536,8 +545,8 @@
             jax.ShapeDtypeStruct((32, 512), F32),
         ),
         in_specs=[
-            vmem,
-            vmem,
+            anywhere,
+            anywhere,
             vmem,
             pl.BlockSpec(memory_space=pltpu.SMEM),
             vmem,
@@ -546,6 +555,8 @@
         ],
         out_specs=(vmem, vmem),
         scratch_shapes=[
+            pltpu.VMEM((128, 1024), BF16),
+            pltpu.VMEM((128, 1024), BF16),
             pltpu.VMEM((2, 64, 1024), BF16),
             pltpu.VMEM((2, 64, 1024), BF16),
             pltpu.VMEM((128, 1024), F32),
@@ -584,7 +595,7 @@
             pltpu.VMEM((2, 32, 512), BF16),
             pltpu.VMEM((32, 512), BF16),
             pltpu.VMEM((128, 1024), F32),
-            pltpu.SemaphoreType.DMA((2,)),
+            pltpu.SemaphoreType.DMA((4,)),
             pltpu.SemaphoreType.DMA((30,)),
             pltpu.SemaphoreType.DMA((30,)),
             pltpu.SemaphoreType.DMA((14,)),

time: 75.8 us -> 75.6 us (level)
  no operation moved by 1% of the time
where the time goes in v3:
time: 75.6 us; the launch traced here: 75.5 us
  Pallas kernels  74.8 us (99%)
    pallas_call x1, Pallas kernels, shards(): pl.pallas_call(lambda *refs: block_kernel(factor, *refs), out_shape=(jax....  73.2 us
    pallas_call x1, Pallas kernels, shards(): pl.pallas_call(place_results, out_shape=(jax.ShapeDtypeStruct((128, 1024)...  1.68 us

profile of v3, /device:TPU:1, one launch (start us, length us, event | category | flops | bytes accessed | tf_op | source)
XLA Modules:
  0.0 75.5 jit_solution(16232403116757791515)
XLA Ops:
  0.6 73.2 %attention_block_grads.1 = (bf16[128,1024]{1,0:T(8,128)(2,1)}, f32[32,512]{1,0:T(8,128)}) custom-call(bf16[128,1024]{1,0:T(8,128)(2,1)} %bitcast.5, bf16[128,1024]{1,0:T(8,128)(2,1)} %bitcast.6, s32[1,128]{1,0:T(1,128)} %refs_2_.1, s32[1,8]{1,0:T(1,128)} %refs_3_.1, f32[1,1024]{1,0:T(1,128)} %bitcast.7, bf16[3,1024,1024]{2,1,0:T(8,128)(2,1)} %refs_5_.1, ...), custom_call_target="tpu_custom_call" | custom-call | tf_op jit(solution)/shard_map/attention_block_grads/pallas_call | solution.py:541
  73.8 1.7 %place_results.1 = (bf16[128,1024]{1,0:T(8,128)(2,1)}, f32[3,32,128]{2,1,0:T(8,128)}, f32[32,128]{1,0:T(8,128)}) custom-call(bf16[128,1024]{1,0:T(8,128)(2,1)} %get-tuple-element.8.rows_ref, f32[32,512]{1,0:T(8,128)} %get-tuple-element.9.sums_ref), custom_call_target="tpu_custom_call" | custom-call | tf_op jit(solution)/shard_map/place_results/pallas_call | solution.py:611

commit v4 on v3

--- a/solution.py
+++ b/solution.py
@@ -446,9 +446,7 @@
 
     def add_rows(which, block, first=False):
         heads = pl.ds(pl.multiple_of(which * 128, 128), 128)
-        term = dot(block[:, :128], weights[0, heads, :], 1, 0)
-        term = term + dot(block[:, 128:256], weights[1, heads, :], 1, 0)
-        term = term + dot(block[:, 256:], weights[2, heads, :], 1, 0)
+        term = dot(block, weights[:, heads, :].reshape(384, 1024), 1, 0)
         total[...] = term if first else total[...] + term
 
     def came(index, which, columns=rest):

time: 75.6 us -> 75.8 us (level)
  no operation moved by 1% of the time
where the time goes in v4:
time: 75.8 us; the launch traced here: 75.7 us
  Pallas kernels  75 us (99%)
    pallas_call x1, Pallas kernels, shards(): pl.pallas_call(lambda *refs: block_kernel(factor, *refs), out_shape=(jax....  73.3 us
    pallas_call x1, Pallas kernels, shards(): pl.pallas_call(place_results, out_shape=(jax.ShapeDtypeStruct((128, 1024)...  1.68 us

profile of v4, /device:TPU:1, one launch (start us, length us, event | category | flops | bytes accessed | tf_op | source)
XLA Modules:
  0.0 75.7 jit_solution(11316829190458319844)
XLA Ops:
  0.6 73.3 %attention_block_grads.1 = (bf16[128,1024]{1,0:T(8,128)(2,1)}, f32[32,512]{1,0:T(8,128)}) custom-call(bf16[128,1024]{1,0:T(8,128)(2,1)} %bitcast.5, bf16[128,1024]{1,0:T(8,128)(2,1)} %bitcast.6, s32[1,128]{1,0:T(1,128)} %refs_2_.1, s32[1,8]{1,0:T(1,128)} %refs_3_.1, f32[1,1024]{1,0:T(1,128)} %bitcast.7, bf16[3,1024,1024]{2,1,0:T(8,128)(2,1)} %refs_5_.1, ...), custom_call_target="tpu_custom_call" | custom-call | tf_op jit(solution)/shard_map/attention_block_grads/pallas_call | solution.py:539
  74.0 1.7 %place_results.1 = (bf16[128,1024]{1,0:T(8,128)(2,1)}, f32[3,32,128]{2,1,0:T(8,128)}, f32[32,128]{1,0:T(8,128)}) custom-call(bf16[128,1024]{1,0:T(8,128)(2,1)} %get-tuple-element.8.rows_ref, f32[32,512]{1,0:T(8,128)} %get-tuple-element.9.sums_ref), custom_call_target="tpu_custom_call" | custom-call | tf_op jit(solution)/shard_map/place_results/pallas_call | solution.py:609
